TPU v7x, 32 devices: a whole 2x2x4 slice. The times are simulated.
32 devices in a mesh: kpt: 4 (over y, core), row: 4 (over z), col: 2 (over x).
Axes of the slice: x: 2, y: 2, z: 4, core: 2. Of those that a mesh axis runs over, the one named last changes fastest.
Arguments:
- a_matrix: bfloat16 [8, 4096, 4096], P('kpt', 'row', 'col'), parts along dimension 0, may hold values from -6 to 6
- b_matrix: bfloat16 [8, 4096, 4096], P('kpt', 'row', 'col'), parts along dimension 0, may hold values from -0.09375 to 0.09375
- a_level: int32 [128, 32], P('kpt'), parts along dimension 0, may hold values from 0 to 4, as said below
- b_level: int32 [128, 32], P('kpt'), parts along dimension 0, may hold values from 0 to 4, as said below
- limit: int32 [128, 32], P(('kpt', 'row'), 'col'), parts along dimension 0, may hold values from 3 to 8
Outputs:
- product: bfloat16 [8, 4096, 4096], P('kpt', 'row', 'col'), parts along dimension 0
- kept_count: int32 [128, 32], P(('kpt', 'row'), 'col'), parts along dimension 0
- kept_total: int32 [4], P('kpt'), parts along dimension 0
There are 4 independent parts, one for each index of `kpt`. A program takes and returns all parts, laid end to end along the dimension named above; each array names one. Nothing has to cross between parts.
Inputs may be any that keep to these rules, and one draw needn't show every extreme that they name: Each block's level is 0 (empty) or its norm exponent 1 to 4; the share of occupied blocks rises from some a sixth in the first block row of a_level (block column of b_level) to some six in seven in the last. `b_level`: as for a_level, with the share rising along block columns.
All inputs are finite; a program needn't handle non-finite values.
Results may differ from a plain program's by a relative error of at most 0.001.
Values may be sent and summed in bfloat16 or wider, within the bound.
No kernel may reach another device: no remote copies, remote signals or barrier semaphores. Data moves between devices by JAX's collectives and lax.ppermute only.
A program may use at most 576 MiB of HBM per device.

v0:
```python
import jax
import jax.numpy as jnp
from jax import lax
from jax.sharding import PartitionSpec as P

BLK = 128


def level_scale(levels):
    power = jnp.power(jnp.float32(2.0), (1 - levels).astype(jnp.float32))
    return jnp.where(levels > 0, power, jnp.float32(0.0))


def spread_blocks(small):
    return jnp.repeat(jnp.repeat(small, BLK, axis=0), BLK, axis=1)


def block_terms(a_piece, a_lev, b_piece, b_lev, limit):
    keep = (
        (a_lev[:, :, None] > 0)
        & (b_lev[None, :, :] > 0)
        & (a_lev[:, :, None] + b_lev[None, :, :] <= limit[:, None, :])
    )
    counted = jnp.sum(keep.astype(jnp.int32), axis=1)
    results = []
    for column in range(limit.shape[1]):
        mask = jnp.repeat(keep[:, :, column], BLK, axis=0)
        masked = jnp.where(mask[None], a_piece, jnp.zeros((), jnp.bfloat16))
        right = b_piece[:, :, column * BLK : (column + 1) * BLK]
        real_real = jnp.dot(masked[0], right[0], preferred_element_type=jnp.float32)
        imag_imag = jnp.dot(masked[1], right[1], preferred_element_type=jnp.float32)
        real_imag = jnp.dot(masked[0], right[1], preferred_element_type=jnp.float32)
        imag_real = jnp.dot(masked[1], right[0], preferred_element_type=jnp.float32)
        results.append(jnp.stack([real_real - imag_imag, real_imag + imag_real]))
    return (jnp.concatenate(results, axis=2), counted)


def shards(a_matrix, b_matrix, a_level, b_level, limit):
    row_place = lax.axis_index("row")
    col_place = lax.axis_index("col")
    row_blocks = a_matrix.shape[1] // BLK
    col_blocks = a_matrix.shape[2] // BLK
    a_own = lax.dynamic_slice(
        a_level, (row_place * row_blocks, col_place * col_blocks), (row_blocks, col_blocks)
    )
    b_own = lax.dynamic_slice(
        b_level, (row_place * row_blocks, col_place * col_blocks), (row_blocks, col_blocks)
    )
    a_eff = a_matrix * spread_blocks(level_scale(a_own)).astype(jnp.bfloat16)[None]
    b_eff = b_matrix * spread_blocks(level_scale(b_own)).astype(jnp.bfloat16)[None]
    a_band = lax.dynamic_slice_in_dim(a_level, row_place * row_blocks, row_blocks, 0)
    b_band = lax.dynamic_slice_in_dim(b_level, col_place * col_blocks, col_blocks, 1)
    a_levels = jnp.repeat(a_band, BLK, axis=1)
    b_levels = jnp.repeat(b_band, BLK, axis=0)
    a_whole = lax.all_gather(a_eff, "col", axis=2, tiled=True)
    added, counted = block_terms(
        a_whole, a_levels, lax.all_gather(b_eff, "row", axis=1, tiled=True), b_levels, limit
    )
    kept_count = counted // BLK
    kept_total = lax.psum(jnp.sum(kept_count).reshape(1), ("row", "col"))
    return (added.astype(jnp.bfloat16), kept_count, kept_total)


def solution(mesh):
    in_specs = (
        P("kpt", "row", "col"),
        P("kpt", "row", "col"),
        P("kpt", None),
        P("kpt", None),
        P(("kpt", "row"), "col"),
    )
    out_specs = (P("kpt", "row", "col"), P(("kpt", "row"), "col"), P("kpt"))
    return jax.shard_map(shards, mesh=mesh, in_specs=in_specs, out_specs=out_specs, check_vma=False)
```

profile of v0, /device:TPU:0, one launch (start us, length us, event | category | flops | bytes accessed | tf_op | source)
XLA Modules:
  0.0 1229.6 jit_solution(12622931891409190300)
XLA Ops:
  25.3 8.4 broadcast_multiply_fusion
  37.7 14.6 %psum.7 = s32[1]{0:T(128)} all-reduce(s32[1]{0:T(128)} %bitcast.131), channel_id=1, replica_groups=mesh['kpt'=4,'row'=4,'col'=2] {'row','col'}, use_global_device_ids=true, to_apply=%region_2.3 | all-reduce | flops 1 | bytes 8 | tf_op jit(solution)/shard_map/psum | solution.py:60
  52.3 168.1 %all-gather.3.cloned.1.call-done = bf16[2,1024,4096]{2,1,0:T(8,128)(2,1)} async-done(((bf16[2,1024,2048]{2,1,0:T(8,128)(2,1)}), bf16[2,1024,4096]{2,1,0:T(8,128)(2,1)}) %all-gather.3.cloned.1.call-update) | async-done | bytes 16777232 | tf_op jit(solution)/shard_map/all_gather | solution.py:55
  285.2 115.4 %broadcast_select_fusion = (bf16[2,1024,4096]{2,1,0:T(8,128)(2,1)}, bf16[2,1024,4096]{2,1,0:T(8,128)(2,1)}, bf16[2,1024,4096]{2,1,0:T(8,128)(2,1)}, bf16[2,1024,...) fusion(bf16[2,1024,4096]{2,1,0:T(8,128)(2,1)} %all-gather.3.clo, ...), kind=kLoop, calls=%fused_computation | loop fusion | flops 134217728 | bytes 352321536 | tf_op jit(solution)/shard_map/jit(_where)/select_n | solution.py:28
  400.6 382.8 %all-gather.5.cloned.1.call-done = bf16[2,4096,2048]{2,1,0:T(8,128)(2,1)} async-done(((bf16[2,1024,2048]{2,1,0:T(8,128)(2,1)}), bf16[2,4096,2048]{2,1,0:T(8,128)(2,1)}) %all-gather.5.cloned.1.call-update) | async-done | bytes 33554448 | tf_op jit(solution)/shard_map/all_gather | solution.py:57
  783.4 6.7 fusion.1
  811.6 6.5 fusion.4
  818.1 6.7 fusion.157
  824.8 6.5 fusion.158
  838.6 6.5 fusion.8
  845.2 6.5 fusion.155
  851.7 6.5 fusion.156
  859.0 6.7 fusion.13
  865.8 6.5 fusion.12
  872.3 6.5 fusion.153
  878.8 6.5 fusion.154
  892.6 6.5 fusion.16
  899.2 6.9 fusion.151
  906.1 6.5 fusion.152
  919.9 6.5 fusion.20
  926.5 6.5 fusion.149
  933.0 6.5 fusion.150
  940.3 6.7 fusion.25
  947.0 6.5 fusion.24
  953.5 6.5 fusion.147
  960.0 6.5 fusion.148
  973.9 6.5 fusion.28
  980.4 6.7 fusion.145
  987.1 6.5 fusion.146
  1001.0 6.5 fusion.32
  1007.5 6.5 fusion.143
  1021.3 6.9 fusion.37
  1028.2 6.5 fusion.36
  1034.7 6.5 fusion.141
  1055.1 6.5 fusion.40
  1061.7 6.7 fusion.139
  1082.2 6.5 fusion.44
  1088.7 6.5 fusion.137
  1102.6 6.7 fusion.49
  1109.3 6.5 fusion.48
  1115.8 6.5 fusion.135
  1136.2 6.5 fusion.52
  1142.7 6.9 fusion.133
  1163.4 6.5 fusion.56
  1170.0 6.5 fusion.131
  1190.3 6.7 fusion.60
  1197.0 6.5 fusion.129
  1210.9 11.6 copy.28
  (88 shorter events, 237.9 us)
Async XLA Ops:
  7.2 213.3 %all-gather.3.cloned.1.call-start = ((), (), s32[]{:S(2)}) async-start(), calls=%async_computation | async-start | bytes 25165824 | tf_op jit(solution)/shard_map/all_gather | solution.py:55
  7.2 7.6 copy-start.1
  18.6 764.8 %all-gather.5.cloned.1.call-start = ((), (), s32[]{:S(2)}) async-start(), calls=%async_computation.1 | async-start | bytes 41943040 | tf_op jit(solution)/shard_map/all_gather | solution.py:57
  25.3 8.4 copy-start.2
  25.3 9.6 copy-start.3
  783.4 8.5 copy-start
Sparse Core Ops, SparseCore 0:
  18.7 201.6 all-gather.2
  222.0 561.3 all-gather.4
where the time goes:
time: 1240 us; the launch traced here: 1230 us
  waiting for transfers between devices  551 us (44%)
  matrix products  412 us (33%)
  other arithmetic  144 us (12%)
  local copies, waits for them, and re-layouts  92.9 us (7%)
  between operations  14.8 us (1%)
  blocking collectives  14.6 us (1%)
    all_gather x1, waiting for transfers between devices, shards(): lax.all_gather(b_eff, 'row', axis=1, tiled=True)  383 us
    all_gather x1, waiting for transfers between devices, shards(): a_whole = lax.all_gather(a_eff, 'col', axis=2, tiled=True)  168 us
    select_n x1, other arithmetic, block_terms(): masked = jnp.where(mask[None], a_piece, jnp.zeros((), jnp.bfloat16))  115 us
    dot_general x16, matrix products, block_terms(): real_real = jnp.dot(masked[0], right[0], preferred_element_type=jnp.float32)  105 us
    dot_general x16, matrix products, block_terms(): imag_imag = jnp.dot(masked[1], right[1], preferred_element_type=jnp.float32)  103 us
    dot_general x16, matrix products, block_terms(): real_imag = jnp.dot(masked[0], right[1], preferred_element_type=jnp.float32)  102 us
    dot_general x16, matrix products, block_terms(): imag_real = jnp.dot(masked[1], right[0], preferred_element_type=jnp.float32)  102 us
    broadcast_in_dim x16, local copies, waits for them, and re-layouts, block_terms(): mask = jnp.repeat(keep[:, :, column], BLK, axis=0)  64.8 us
  transfers between devices with their start and end apart: 2, of which 2 were waited for; matrix products, arithmetic and copies ran while one was open for 16% of the time, Pallas kernels for 0%

commit v1 on v0

--- a/solution.py
+++ b/solution.py
@@ -2,8 +2,31 @@
 import jax.numpy as jnp
 from jax import lax
 from jax.sharding import PartitionSpec as P
+from jax.lax import axis_index, axis_size, ppermute
 
 BLK = 128
+
+
+def enter_outputs(vals, which_axis):
+    taken_in = axis_size(which_axis)
+    n_now, piece_now, after = (taken_in, axis_index(which_axis), vals.shape[1])
+    copies = tuple(((dd, (dd + 1) % n_now) for dd in range(n_now)))
+    tray = tuple(((dd, (dd - 1) % n_now) for dd in range(n_now)))
+    item_now = jnp.zeros((*vals.shape[:1], n_now * after, *vals.shape[2:]), vals.dtype)
+    item_now = lax.dynamic_update_slice_in_dim(item_now, vals, piece_now * after, axis=1)
+    known = right_arr = vals
+    x_new = n_now // 2
+    for p in tuple(range(1, x_new + 1)):
+        known = ppermute(known, which_axis, copies)
+        item_now = lax.dynamic_update_slice_in_dim(
+            item_now, known, (piece_now - p) % n_now * after, axis=1
+        )
+        if p < n_now - x_new:
+            right_arr = ppermute(right_arr, which_axis, tray)
+            item_now = lax.dynamic_update_slice_in_dim(
+                item_now, right_arr, (piece_now + p) % n_now * after, axis=1
+            )
+    return item_now
 
 
 def level_scale(levels):
@@ -53,9 +76,7 @@
     a_levels = jnp.repeat(a_band, BLK, axis=1)
     b_levels = jnp.repeat(b_band, BLK, axis=0)
     a_whole = lax.all_gather(a_eff, "col", axis=2, tiled=True)
-    added, counted = block_terms(
-        a_whole, a_levels, lax.all_gather(b_eff, "row", axis=1, tiled=True), b_levels, limit
-    )
+    added, counted = block_terms(a_whole, a_levels, enter_outputs(b_eff, "row"), b_levels, limit)
     kept_count = counted // BLK
     kept_total = lax.psum(jnp.sum(kept_count).reshape(1), ("row", "col"))
     return (added.astype(jnp.bfloat16), kept_count, kept_total)

time: 1240 us -> 1230 us (level)
  waiting for transfers between devices: 551 us -> 171 us
  blocking collectives: 14.6 us -> 357 us
  local copies, waits for them, and re-layouts: 92.9 us -> 132 us
  matrix products: 412 us -> 392 us
    all_gather x1 -> x0, waiting for transfers between devices: 383 us -> none  [shards(): lax.all_gather(b_eff, 'row', axis=1, tiled=True)]
    psum x1, blocking collectives: 14.6 us -> 357 us  [shards(): kept_total = lax.psum(jnp.sum(kept_count).reshape(1), ('row', 'col'))]
    ppermute x0 -> x3, waiting for transfers between devices: none -> 171 us  [the longest x2 171 us: enter_outputs(): known = ppermute(known, which_axis, copies)]
    all_gather x1, waiting for transfers between devices: 168 us -> 0.01 us  [shards(): a_whole = lax.all_gather(a_eff, 'col', axis=2, tiled=True)]
    dynamic_update_slice x0 -> x3, local copies, waits for them, and re-layouts: none -> 25.2 us  [the longest x2 16.7 us: enter_outputs(): lax.dynamic_update_slice_in_dim(item_now, known, (piece_now - p) % n_now...]
    broadcast_in_dim x0 -> x1, local copies, waits for them, and re-layouts: none -> 13.1 us  [enter_outputs(): jnp.zeros((*vals.shape[:1], n_now * after, *vals.shape[2:]), vals.dtype)]
  transfers between devices with their start and end apart: 2 -> 4, of which waited for: 2 -> 1; matrix products, arithmetic and copies ran while one was open for 16% -> 3% of each run, Pallas kernels for 0% -> 0%
where the time goes in v1:
time: 1230 us; the launch traced here: 1220 us
  matrix products  392 us (32%)
  blocking collectives  357 us (29%)
  waiting for transfers between devices  171 us (14%)
  other arithmetic  146 us (12%)
  local copies, waits for them, and re-layouts  132 us (11%)
  between operations  15.7 us (1%)
    psum x1, blocking collectives, shards(): kept_total = lax.psum(jnp.sum(kept_count).reshape(1), ('row', 'col'))  357 us
    ppermute x2, waiting for transfers between devices, enter_outputs(): known = ppermute(known, which_axis, copies)  171 us
    select_n x1, other arithmetic, block_terms(): masked = jnp.where(mask[None], a_piece, jnp.zeros((), jnp.bfloat16))  115 us
    dot_general x16, matrix products, block_terms(): imag_imag = jnp.dot(masked[1], right[1], preferred_element_type=jnp.float32)  104 us
    dot_general x16, matrix products, block_terms(): real_real = jnp.dot(masked[0], right[0], preferred_element_type=jnp.float32)  99.3 us
    dot_general x16, matrix products, block_terms(): imag_real = jnp.dot(masked[1], right[0], preferred_element_type=jnp.float32)  96.1 us
    dot_general x16, matrix products, block_terms(): real_imag = jnp.dot(masked[0], right[1], preferred_element_type=jnp.float32)  92 us
    broadcast_in_dim x16, local copies, waits for them, and re-layouts, block_terms(): mask = jnp.repeat(keep[:, :, column], BLK, axis=0)  63.2 us
  transfers between devices with their start and end apart: 4, of which 1 were waited for; matrix products, arithmetic and copies ran while one was open for 3% of the time, Pallas kernels for 0%

profile of v1, /device:TPU:0, one launch (start us, length us, event | category | flops | bytes accessed | tf_op | source)
XLA Modules:
  0.0 1219.5 jit_solution(17507505233976370654)
XLA Ops:
  16.7 13.1 %broadcast_in_dim.220 = bf16[2,4096,2048]{2,1,0:T(8,128)(2,1)} broadcast(bf16[]{:T(256)} %constant.62.clone.1), dimensions={} | broadcast | bytes 33554432 | tf_op jit(solution)/shard_map/broadcast_in_dim | solution.py:15
  29.8 11.0 constant_dynamic-update-slice_fusion.3
  56.4 171.1 %collective-permute-done = bf16[2,1024,2048]{2,1,0:T(8,128)(2,1)} collective-permute-done((bf16[2,1024,2048]{2,1,0:T(8,128)(2,1)}, bf16[2,1024,2048]{2,1,0:T(8,128)(2,1)}, u32[]{:S(2)}, u32[]{:S(2)}) %collective-permute-start) | collective-permute-done | bytes 8388640 | tf_op jit(solution)/shard_map/ppermute | solution.py:20
  231.5 357.4 %psum.7 = s32[1]{0:T(128)} all-reduce(s32[1]{0:T(128)} %bitcast.131), channel_id=1, replica_groups=mesh['kpt'=4,'row'=4,'col'=2] {'row','col'}, use_global_device_ids=true, to_apply=%region_2.3 | all-reduce | flops 1 | bytes 8 | tf_op jit(solution)/shard_map/psum | solution.py:81
  589.0 8.3 constant_dynamic-update-slice_fusion.2
  597.3 8.5 constant_dynamic-update-slice_fusion.1
  605.8 8.4 constant_dynamic-update-slice_fusion
  677.5 114.7 %broadcast_select_fusion = (bf16[2,1024,4096]{2,1,0:T(8,128)(2,1)}, bf16[2,1024,4096]{2,1,0:T(8,128)(2,1)}, bf16[2,1024,4096]{2,1,0:T(8,128)(2,1)}, bf16[2,1024,...) fusion(bf16[2,1024,4096]{2,1,0:T(8,128)(2,1)} %all-gather.2.clo, ...), kind=kLoop, calls=%fused_computation | loop fusion | flops 134217728 | bytes 352321536 | tf_op jit(solution)/shard_map/jit(_where)/select_n | solution.py:51
  792.2 7.5 fusion.2
  805.8 7.5 fusion.6
  813.3 7.5 fusion.7
  825.9 7.5 fusion.11
  843.4 7.5 fusion.18
  850.9 7.5 fusion.19
  858.4 5.1 fusion.22
  863.5 7.5 fusion.23
  871.0 5.1 fusion.26
  881.1 7.5 fusion.30
  888.5 7.4 fusion.31
  901.1 7.5 fusion.35
  908.6 5.3 fusion.38
  918.9 7.5 fusion.42
  926.3 7.5 fusion.43
  939.0 7.5 fusion.47
  956.5 7.5 fusion.54
  964.0 7.5 fusion.55
  976.6 7.5 fusion.59
  984.1 5.2 fusion.62
  994.4 7.4 fusion.160
  1006.7 7.4 fusion.158
  1014.1 6.7 fusion.157
  1025.6 6.7 fusion.155
  1040.7 6.7 fusion.152
  1047.4 6.7 fusion.151
  1058.8 7.5 fusion.149
  1076.1 7.4 fusion.146
  1083.4 7.4 fusion.145
  1090.9 5.3 fusion.144
  1096.2 7.5 fusion.143
  1113.6 7.4 fusion.140
  1121.0 7.4 fusion.139
  1128.4 5.5 fusion.138
  1134.0 7.5 fusion.137
  1151.3 7.4 fusion.134
  1158.7 7.4 fusion.133
  1166.1 5.3 fusion.132
  1171.4 6.8 fusion.131
  1200.9 11.6 copy.28
  (379 shorter events, 228.2 us)
Async XLA Ops:
  7.2 607.1 %all-gather.2.cloned.1.call-start = ((), (), s32[]{:S(2)}) async-start(), calls=%async_computation | async-start | bytes 25165824 | tf_op jit(solution)/shard_map/all_gather | solution.py:78
  16.6 13.2 %copy-start = (bf16[128,8,16,128]{3,1,2,0:T(8,128)(2,1)S(1)}, bf16[128,8,16,128]{3,1,2,0:T(8,128)(2,1)}, u32[]{:S(2)}) copy-start(bf16[128,8,16,128]{3,1,2,0:T(8,128)(2,1)} %copy.37) | copy-start | bytes 12582916
  16.6 34.0 %slice-start.84 = ((s8[8388608]{0:T(1024)(128)(4,1)}), s8[4194304]{0:T(1024)(128)(4,1)S(1)}, s32[]{:S(2)}) async-start(s8[8388608]{0:T(1024)(128)(4,1)} %bitcast.644), calls=%async_computation.85 | async-start | bytes 8388608
  29.8 20.9 %slice-start.85 = ((s8[8388608]{0:T(1024)(128)(4,1)}), s8[4194304]{0:T(1024)(128)(4,1)S(1)}, s32[]{:S(2)}) async-start(s8[8388608]{0:T(1024)(128)(4,1)} %bitcast.644), calls=%async_computation.86 | async-start | bytes 8388608
  40.8 186.7 %collective-permute-start = (bf16[2,1024,2048]{2,1,0:T(8,128)(2,1)}, bf16[2,1024,2048]{2,1,0:T(8,128)(2,1)}, u32[]{:S(2)}, u32[]{:S(2)}) collective-permute-start(bf16[2,1024,2048]{2,1,0:T(8,128)(2,1)} %get-tuple-element.17), channel_id=1, source_target_pairs={{0,2},{2,4},{4,6},{6,0},{1,3},{3,5},{5,7},{7,1},{8,10},{10,12},{12... | collective-permute-start | bytes 25165832 | tf_op jit(solution)/shard_map/ppermute | solution.py:20
  50.6 177.0 %copy-start.24 = (s32[8,16]{1,0:T(8,128)S(1)}, s32[8,16]{1,0:T(8,128)}, u32[]{:S(2)}) copy-start(s32[8,16]{1,0:T(8,128)} %param.9) | copy-start | bytes 1540
  50.6 177.1 %copy-start.23 = (s32[32,32]{1,0:T(8,128)S(1)}, s32[32,32]{1,0:T(8,128)}, u32[]{:S(2)}) copy-start(s32[32,32]{1,0:T(8,128)} %param.8) | copy-start | bytes 12292
  54.5 542.8 %collective-permute-start.1 = (bf16[2,1024,2048]{2,1,0:T(8,128)(2,1)}, bf16[2,1024,2048]{2,1,0:T(8,128)(2,1)}, u32[]{:S(2)}, u32[]{:S(2)}) collective-permute-start(bf16[2,1024,2048]{2,1,0:T(8,128)(2,1)} %get-tuple-element.17), channel_id=1, source_target_pairs={{0,6},{2,0},{4,2},{6,4},{1,7},{3,1},{5,3},{7,5},{8,14},{10,8},{12,... | collective-permute-start | bytes 25165832 | tf_op jit(solution)/shard_map/ppermute | solution.py:25
  227.5 378.3 %collective-permute-start.2 = (bf16[2,1024,2048]{2,1,0:T(8,128)(2,1)}, bf16[2,1024,2048]{2,1,0:T(8,128)(2,1)}, u32[]{:S(2)}, u32[]{:S(2)}) collective-permute-start(bf16[2,1024,2048]{2,1,0:T(8,128)(2,1)} %collective-permute-done), channel_id=1, source_target_pairs={{0,2},{2,4},{4,6},{6,0},{1,3},{3,5},{5,7},{7,1},{8,10},{10,12},{12... | collective-permute-start | bytes 25165832 | tf_op jit(solution)/shard_map/ppermute | solution.py:20
  805.8 15.0 %slice-start.72 = ((s8[16777216]{0:T(1024)(128)(4,1)}), s8[4194304]{0:T(1024)(128)(4,1)S(1)}, s32[]{:S(2)}) async-start(s8[16777216]{0:T(1024)(128)(4,1)} %bitcast.638), calls=%async_computation.73 | async-start | bytes 8388608
  805.8 15.0 %slice-start.73 = ((s8[16777216]{0:T(1024)(128)(4,1)}), s8[4194304]{0:T(1024)(128)(4,1)S(1)}, s32[]{:S(2)}) async-start(s8[16777216]{0:T(1024)(128)(4,1)} %bitcast.638), calls=%async_computation.74 | async-start | bytes 8388608
  820.7 12.6 %slice-start.64 = ((s8[16777216]{0:T(1024)(128)(4,1)}), s8[4194304]{0:T(1024)(128)(4,1)S(1)}, s32[]{:S(2)}) async-start(s8[16777216]{0:T(1024)(128)(4,1)} %bitcast.634), calls=%async_computation.65 | async-start | bytes 8388608
  843.4 15.0 %slice-start.56 = ((s8[16777216]{0:T(1024)(128)(4,1)}), s8[4194304]{0:T(1024)(128)(4,1)S(1)}, s32[]{:S(2)}) async-start(s8[16777216]{0:T(1024)(128)(4,1)} %bitcast.630), calls=%async_computation.57 | async-start | bytes 8388608
  843.4 15.0 %slice-start.57 = ((s8[16777216]{0:T(1024)(128)(4,1)}), s8[4194304]{0:T(1024)(128)(4,1)S(1)}, s32[]{:S(2)}) async-start(s8[16777216]{0:T(1024)(128)(4,1)} %bitcast.630), calls=%async_computation.58 | async-start | bytes 8388608
  858.4 12.6 %slice-start.48 = ((s8[16777216]{0:T(1024)(128)(4,1)}), s8[4194304]{0:T(1024)(128)(4,1)S(1)}, s32[]{:S(2)}) async-start(s8[16777216]{0:T(1024)(128)(4,1)} %bitcast.626), calls=%async_computation.49 | async-start | bytes 8388608
  858.4 12.6 %slice-start.49 = ((s8[16777216]{0:T(1024)(128)(4,1)}), s8[4194304]{0:T(1024)(128)(4,1)S(1)}, s32[]{:S(2)}) async-start(s8[16777216]{0:T(1024)(128)(4,1)} %bitcast.626), calls=%async_computation.50 | async-start | bytes 8388608
  881.1 14.9 %slice-start.40 = ((s8[16777216]{0:T(1024)(128)(4,1)}), s8[4194304]{0:T(1024)(128)(4,1)S(1)}, s32[]{:S(2)}) async-start(s8[16777216]{0:T(1024)(128)(4,1)} %bitcast.622), calls=%async_computation.41 | async-start | bytes 8388608
  881.1 14.9 %slice-start.41 = ((s8[16777216]{0:T(1024)(128)(4,1)}), s8[4194304]{0:T(1024)(128)(4,1)S(1)}, s32[]{:S(2)}) async-start(s8[16777216]{0:T(1024)(128)(4,1)} %bitcast.622), calls=%async_computation.42 | async-start | bytes 8388608
  918.9 14.9 %slice-start.24 = ((s8[16777216]{0:T(1024)(128)(4,1)}), s8[4194304]{0:T(1024)(128)(4,1)S(1)}, s32[]{:S(2)}) async-start(s8[16777216]{0:T(1024)(128)(4,1)} %bitcast.614), calls=%async_computation.25 | async-start | bytes 8388608
  918.9 14.9 %slice-start.25 = ((s8[16777216]{0:T(1024)(128)(4,1)}), s8[4194304]{0:T(1024)(128)(4,1)S(1)}, s32[]{:S(2)}) async-start(s8[16777216]{0:T(1024)(128)(4,1)} %bitcast.614), calls=%async_computation.26 | async-start | bytes 8388608
  933.8 12.6 %slice-start.16 = ((s8[16777216]{0:T(1024)(128)(4,1)}), s8[4194304]{0:T(1024)(128)(4,1)S(1)}, s32[]{:S(2)}) async-start(s8[16777216]{0:T(1024)(128)(4,1)} %bitcast.610), calls=%async_computation.17 | async-start | bytes 8388608
  956.5 15.0 %slice-start.8 = ((s8[16777216]{0:T(1024)(128)(4,1)}), s8[4194304]{0:T(1024)(128)(4,1)S(1)}, s32[]{:S(2)}) async-start(s8[16777216]{0:T(1024)(128)(4,1)} %bitcast.606), calls=%async_computation.9 | async-start | bytes 8388608
  956.5 15.0 %slice-start.9 = ((s8[16777216]{0:T(1024)(128)(4,1)}), s8[4194304]{0:T(1024)(128)(4,1)S(1)}, s32[]{:S(2)}) async-start(s8[16777216]{0:T(1024)(128)(4,1)} %bitcast.606), calls=%async_computation.10 | async-start | bytes 8388608
  1006.7 14.1 %slice-start.76 = ((s8[16777216]{0:T(1024)(128)(4,1)}), s8[4194304]{0:T(1024)(128)(4,1)S(1)}, s32[]{:S(2)}) async-start(s8[16777216]{0:T(1024)(128)(4,1)} %bitcast.640), calls=%async_computation.77 | async-start | bytes 8388608
  1006.7 14.1 %slice-start.77 = ((s8[16777216]{0:T(1024)(128)(4,1)}), s8[4194304]{0:T(1024)(128)(4,1)S(1)}, s32[]{:S(2)}) async-start(s8[16777216]{0:T(1024)(128)(4,1)} %bitcast.640), calls=%async_computation.78 | async-start | bytes 8388608
  1006.7 14.1 %copy-start.44 = (f32[1024,128]{0,1:T(8,128)S(1)}, f32[1024,128]{0,1:T(8,128)}, u32[]{:S(2)}) copy-start(f32[1024,128]{0,1:T(8,128)} %fusion.10) | copy-start | bytes 1572868
  1040.7 13.4 %slice-start.60 = ((s8[16777216]{0:T(1024)(128)(4,1)}), s8[4194304]{0:T(1024)(128)(4,1)S(1)}, s32[]{:S(2)}) async-start(s8[16777216]{0:T(1024)(128)(4,1)} %bitcast.632), calls=%async_computation.61 | async-start | bytes 8388608
  1040.7 13.4 %slice-start.61 = ((s8[16777216]{0:T(1024)(128)(4,1)}), s8[4194304]{0:T(1024)(128)(4,1)S(1)}, s32[]{:S(2)}) async-start(s8[16777216]{0:T(1024)(128)(4,1)} %bitcast.632), calls=%async_computation.62 | async-start | bytes 8388608
  1076.1 14.8 %slice-start.44 = ((s8[16777216]{0:T(1024)(128)(4,1)}), s8[4194304]{0:T(1024)(128)(4,1)S(1)}, s32[]{:S(2)}) async-start(s8[16777216]{0:T(1024)(128)(4,1)} %bitcast.624), calls=%async_computation.45 | async-start | bytes 8388608
  1076.1 14.8 %slice-start.45 = ((s8[16777216]{0:T(1024)(128)(4,1)}), s8[4194304]{0:T(1024)(128)(4,1)S(1)}, s32[]{:S(2)}) async-start(s8[16777216]{0:T(1024)(128)(4,1)} %bitcast.624), calls=%async_computation.46 | async-start | bytes 8388608
  1090.9 12.9 %slice-start.36 = ((s8[16777216]{0:T(1024)(128)(4,1)}), s8[4194304]{0:T(1024)(128)(4,1)S(1)}, s32[]{:S(2)}) async-start(s8[16777216]{0:T(1024)(128)(4,1)} %bitcast.620), calls=%async_computation.37 | async-start | bytes 8388608
  1090.9 12.9 %slice-start.37 = ((s8[16777216]{0:T(1024)(128)(4,1)}), s8[4194304]{0:T(1024)(128)(4,1)S(1)}, s32[]{:S(2)}) async-start(s8[16777216]{0:T(1024)(128)(4,1)} %bitcast.620), calls=%async_computation.38 | async-start | bytes 8388608
  1113.6 14.8 %slice-start.28 = ((s8[16777216]{0:T(1024)(128)(4,1)}), s8[4194304]{0:T(1024)(128)(4,1)S(1)}, s32[]{:S(2)}) async-start(s8[16777216]{0:T(1024)(128)(4,1)} %bitcast.616), calls=%async_computation.29 | async-start | bytes 8388608
  1113.6 14.8 %slice-start.29 = ((s8[16777216]{0:T(1024)(128)(4,1)}), s8[4194304]{0:T(1024)(128)(4,1)S(1)}, s32[]{:S(2)}) async-start(s8[16777216]{0:T(1024)(128)(4,1)} %bitcast.616), calls=%async_computation.30 | async-start | bytes 8388608
  1128.4 13.1 %slice-start.20 = ((s8[16777216]{0:T(1024)(128)(4,1)}), s8[4194304]{0:T(1024)(128)(4,1)S(1)}, s32[]{:S(2)}) async-start(s8[16777216]{0:T(1024)(128)(4,1)} %bitcast.612), calls=%async_computation.21 | async-start | bytes 8388608
  1128.4 13.1 %slice-start.21 = ((s8[16777216]{0:T(1024)(128)(4,1)}), s8[4194304]{0:T(1024)(128)(4,1)S(1)}, s32[]{:S(2)}) async-start(s8[16777216]{0:T(1024)(128)(4,1)} %bitcast.612), calls=%async_computation.22 | async-start | bytes 8388608
  1151.3 14.8 %slice-start.12 = ((s8[16777216]{0:T(1024)(128)(4,1)}), s8[4194304]{0:T(1024)(128)(4,1)S(1)}, s32[]{:S(2)}) async-start(s8[16777216]{0:T(1024)(128)(4,1)} %bitcast.608), calls=%async_computation.13 | async-start | bytes 8388608
  1151.3 14.8 %slice-start.13 = ((s8[16777216]{0:T(1024)(128)(4,1)}), s8[4194304]{0:T(1024)(128)(4,1)S(1)}, s32[]{:S(2)}) async-start(s8[16777216]{0:T(1024)(128)(4,1)} %bitcast.608), calls=%async_computation.14 | async-start | bytes 8388608
  1178.3 12.9 %copy-start.5 = (bf16[1,1024,128]{1,2,0:T(8,128)(2,1)S(1)}, bf16[1,1024,128]{1,2,0:T(8,128)(2,1)}, u32[]{:S(2)}) copy-start(bf16[1,1024,128]{1,2,0:T(8,128)(2,1)} %fusion.149) | copy-start | bytes 786436
  1182.6 13.1 %copy-start.14 = (bf16[1,1024,128]{1,2,0:T(8,128)(2,1)S(1)}, bf16[1,1024,128]{1,2,0:T(8,128)(2,1)}, u32[]{:S(2)}) copy-start(bf16[1,1024,128]{1,2,0:T(8,128)(2,1)} %fusion.140) | copy-start | bytes 786436
  1182.6 13.0 %copy-start.15 = (bf16[1,1024,128]{1,2,0:T(8,128)(2,1)S(1)}, bf16[1,1024,128]{1,2,0:T(8,128)(2,1)}, u32[]{:S(2)}) copy-start(bf16[1,1024,128]{1,2,0:T(8,128)(2,1)} %fusion.139) | copy-start | bytes 786436
  1182.6 13.9 %copy-start.16 = (bf16[1,1024,128]{1,2,0:T(8,128)(2,1)S(1)}, bf16[1,1024,128]{1,2,0:T(8,128)(2,1)}, u32[]{:S(2)}) copy-start(bf16[1,1024,128]{1,2,0:T(8,128)(2,1)} %fusion.138) | copy-start | bytes 786436
  1182.6 13.9 %copy-start.17 = (bf16[1,1024,128]{1,2,0:T(8,128)(2,1)S(1)}, bf16[1,1024,128]{1,2,0:T(8,128)(2,1)}, u32[]{:S(2)}) copy-start(bf16[1,1024,128]{1,2,0:T(8,128)(2,1)} %fusion.137) | copy-start | bytes 786436
  1182.7 14.8 %copy-start.18 = (bf16[1,1024,128]{1,2,0:T(8,128)(2,1)S(1)}, bf16[1,1024,128]{1,2,0:T(8,128)(2,1)}, u32[]{:S(2)}) copy-start(bf16[1,1024,128]{1,2,0:T(8,128)(2,1)} %fusion.136) | copy-start | bytes 786436
  1182.7 14.8 %copy-start.19 = (bf16[1,1024,128]{1,2,0:T(8,128)(2,1)S(1)}, bf16[1,1024,128]{1,2,0:T(8,128)(2,1)}, u32[]{:S(2)}) copy-start(bf16[1,1024,128]{1,2,0:T(8,128)(2,1)} %fusion.135) | copy-start | bytes 786436
  1182.7 15.7 %copy-start.20 = (bf16[1,1024,128]{1,2,0:T(8,128)(2,1)S(1)}, bf16[1,1024,128]{1,2,0:T(8,128)(2,1)}, u32[]{:S(2)}) copy-start(bf16[1,1024,128]{1,2,0:T(8,128)(2,1)} %fusion.134) | copy-start | bytes 786436
  1182.7 15.7 %copy-start.21 = (bf16[1,1024,128]{1,2,0:T(8,128)(2,1)S(1)}, bf16[1,1024,128]{1,2,0:T(8,128)(2,1)}, u32[]{:S(2)}) copy-start(bf16[1,1024,128]{1,2,0:T(8,128)(2,1)} %fusion.133) | copy-start | bytes 786436
  1182.7 16.5 %copy-start.22 = (bf16[1,1024,128]{1,2,0:T(8,128)(2,1)S(1)}, bf16[1,1024,128]{1,2,0:T(8,128)(2,1)}, u32[]{:S(2)}) copy-start(bf16[1,1024,128]{1,2,0:T(8,128)(2,1)} %fusion.132) | copy-start | bytes 786436
  (91 other events, 828.5 us)
Sparse Core Ops, SparseCore 0:
  54.6 198.9 all-gather.1
